TPU v7x, 256 devices: a whole 4x4x8 slice. The times are simulated.
256 devices in a mesh: seq: 64 (over z, x, core), head: 4 (over y).
Axes of the slice: x: 4, y: 4, z: 8, core: 2. Of those that a mesh axis runs over, the one named last changes fastest.
Arguments:
- queries: bfloat16 [16384, 4096], P('seq', 'head'), may hold values from -6 to 6
- key_rows: bfloat16 [16384, 4096], P('seq', 'head'), may hold values from -18 to 18
- values: bfloat16 [16384, 4096], P('seq', 'head'), may hold values from -6 to 6
- write_gate: float32 [16384, 32], P('seq', 'head'), may hold values from 0.05 to 1
- ridge_diag: float32 [32, 128], P('head'), may hold values from 0.1 to 4
- norm_gain: float32 [4096], replicated, may hold values from 0.5 to 1.5
- gate_logits: bfloat16 [16384, 4096], P(('seq', 'head')), may hold values from -8 to 8
Outputs:
- layer_out: bfloat16 [16384, 4096], P(('seq', 'head'))
All inputs are finite; a program needn't handle non-finite values.
Results may differ from a plain program's by a relative error of at most 0.018.
Values may be sent and summed in bfloat16 or wider, within the bound.
A program may use at most 128 MiB of HBM per device.

v0:
```python
import jax
import jax.numpy as jnp
from jax import lax
from jax.sharding import PartitionSpec as P

ITERS = 8


precise = lax.Precision.HIGHEST


def prefix(x, axis, combine, identity):
    size, mine = (lax.axis_size(axis), lax.axis_index(axis))
    everything = jax.tree.map(
        lambda part, kind: lax.all_gather(part.astype(kind), axis), x, (jnp.bfloat16, jnp.bfloat16)
    )
    start = jax.tree.map(
        lambda part, zero: jnp.broadcast_to(jnp.asarray(zero, part.dtype), part.shape), x, identity
    )

    def turn(k, before):
        reached = k < mine
        new = combine(
            before, jax.tree.map(lambda part, own: part[k].astype(own.dtype), everything, x)
        )
        return jax.tree.map(lambda a, b: jnp.where(reached, a, b), new, before)

    return lax.fori_loop(0, size, turn, start)


def normalize(block):
    return block * lax.rsqrt(jnp.sum(block * block, axis=-1, keepdims=True) + 1e-06)


def add_pair(earlier, later):
    return (earlier[0] + later[0], earlier[1] + later[1])


def conj_grad(prev_kk, query_n, key_n, weights, ridge_diag):
    iterate = jnp.zeros_like(query_n)
    residual = query_n
    direction = query_n
    norm_now = jnp.sum(residual * residual, axis=-1, keepdims=True)
    for sweep in range(ITERS):
        scores = jnp.einsum("htd,hsd->hts", direction, key_n, precision=precise)
        inner = jnp.einsum("hts,hsd->htd", weights * scores, key_n, precision=precise)
        carried = jnp.einsum("htd,hde->hte", direction, prev_kk, precision=precise)
        image = carried + inner + ridge_diag[:, None, :] * direction
        alpha = norm_now / jnp.sum(direction * image, axis=-1, keepdims=True)
        iterate = iterate + alpha * direction
        residual = residual - alpha * image
        norm_next = jnp.sum(residual * residual, axis=-1, keepdims=True)
        direction = residual + norm_next / norm_now * direction
        norm_now = norm_next
    return iterate


def shards(queries, key_rows, values, write_gate, ridge_diag, norm_gain, gate_logits):
    tok_rows = queries.shape[0]
    heads_here = write_gate.shape[1]
    head_width = queries.shape[1] // heads_here

    def split_heads(block):
        return (
            block.astype(jnp.float32).reshape(tok_rows, heads_here, head_width).transpose(1, 0, 2)
        )

    query_n = normalize(split_heads(queries))
    key_n = normalize(split_heads(key_rows))
    value_f = split_heads(values)
    gate_heads = write_gate.T
    causal = jnp.arange(tok_rows)[:, None] >= jnp.arange(tok_rows)[None, :]
    weights = jnp.where(causal[None, :, :], gate_heads[:, None, :], jnp.float32(0.0))
    local_kk = jnp.einsum("htd,hte->hde", key_n * gate_heads[:, :, None], key_n, precision=precise)
    local_vk = jnp.einsum(
        "htv,htd->hvd", value_f * gate_heads[:, :, None], key_n, precision=precise
    )
    empty_state = jnp.zeros_like(local_kk)
    prev_kk, prev_vk = prefix((local_kk, local_vk), "seq", add_pair, (empty_state, empty_state))
    solution = conj_grad(prev_kk, query_n, key_n, weights, ridge_diag)
    scores = jnp.einsum("htd,hsd->hts", solution, key_n, precision=precise)
    mesa_f = jnp.einsum("htd,hvd->htv", solution, prev_vk, precision=precise)
    mesa_f = mesa_f + jnp.einsum("hts,hsv->htv", weights * scores, value_f, precision=precise)
    mesa_out = (
        mesa_f.transpose(1, 0, 2).reshape(tok_rows, heads_here * head_width).astype(jnp.bfloat16)
    )
    token_block = lax.all_to_all(mesa_out, "head", split_axis=0, concat_axis=1, tiled=True)
    wide_rows = token_block.astype(jnp.float32)
    factor = lax.rsqrt(jnp.mean(wide_rows * wide_rows, axis=-1, keepdims=True) + 1e-06)
    gated = (
        wide_rows * factor * norm_gain[None, :] * jax.nn.sigmoid(gate_logits.astype(jnp.float32))
    )
    return gated.astype(jnp.bfloat16)


def solution(mesh):
    return jax.shard_map(
        shards,
        mesh=mesh,
        in_specs=(
            P("seq", "head"),
            P("seq", "head"),
            P("seq", "head"),
            P("seq", "head"),
            P("head", None),
            P(),
            P(("seq", "head"), None),
        ),
        out_specs=P(("seq", "head"), None),
        check_vma=False,
    )
```

profile of v0, /device:TPU:1, one launch (start us, length us, event | category | flops | bytes accessed | tf_op | source)
XLA Modules:
  0.0 391.8 jit_solution(17072188765604343334)
XLA Ops:
  8.4 3.6 fusion.31
  12.1 3.3 convolution_convert_fusion
  15.5 3.6 fusion.67
  19.0 97.1 %all-gather.5.cloned.1.call-done = bf16[512,128,128]{2,1,0:T(8,128)(2,1)} async-done(((bf16[8,128,128]{2,1,0:T(8,128)(2,1)}), bf16[512,128,128]{2,1,0:T(8,128)(2,1)}) %all-gather.5.cloned.1.call-update) | async-done | bytes 16777232 | tf_op jit(solution)/shard_map/all_gather | solution.py:15
  116.1 99.5 %all-gather.7.cloned.1.call-done = bf16[512,128,128]{2,1,0:T(8,128)(2,1)} async-done(((bf16[8,128,128]{2,1,0:T(8,128)(2,1)}), bf16[512,128,128]{2,1,0:T(8,128)(2,1)}) %all-gather.7.cloned.1.call-update) | async-done | bytes 16777232 | tf_op jit(solution)/shard_map/all_gather | solution.py:15
  215.6 96.0 %while.16 = (s32[]{:T(128)}, f32[8,128,128]{2,1,0:T(8,128)S(1)}, f32[8,128,128]{2,1,0:T(8,128)S(1)}, s32[]{:T(128)}, bf16[64,8,128,128]{3,2,1,0:T(8,128)(2,1)}, ...) while((s32[]{:T(128)}, f32[8,128,128]{2,1,0:T(8,128)S(1)}, ...), condition=%wide.region_4.5_spmd.clone, body=%wide.region_3.4_spmd.clone.sunk | while | flops 1048580 | bytes 2621549 | solution.py:28
  217.1 1.5 add_select_fusion.3
  224.6 1.5 add_select_fusion.3
  226.1 1.5 add_select_fusion.3
  227.6 1.5 add_select_fusion.3
  229.1 1.5 add_select_fusion.3
  230.6 1.5 add_select_fusion.3
  239.6 1.5 add_select_fusion.3
  241.1 1.5 add_select_fusion.3
  242.6 1.5 add_select_fusion.3
  244.1 1.5 add_select_fusion.3
  245.5 1.5 add_select_fusion.3
  253.0 1.5 add_select_fusion.3
  254.5 1.5 add_select_fusion.3
  256.0 1.5 add_select_fusion.3
  257.5 1.5 add_select_fusion.3
  259.0 1.5 add_select_fusion.3
  268.0 1.5 add_select_fusion.3
  269.5 1.5 add_select_fusion.3
  271.0 1.5 add_select_fusion.3
  272.5 1.5 add_select_fusion.3
  274.0 1.5 add_select_fusion.3
  281.5 1.5 add_select_fusion.3
  283.0 1.5 add_select_fusion.3
  284.5 1.5 add_select_fusion.3
  313.2 2.7 multiply_reduce_fusion.13
  316.3 2.2 fusion.105
  319.7 2.5 multiply_reduce_fusion.11
  322.9 2.7 fusion.102
  326.8 2.6 multiply_reduce_fusion.9
  329.7 2.3 fusion.99
  333.2 2.5 multiply_reduce_fusion.7
  336.1 2.5 fusion.96
  339.7 2.5 multiply_reduce_fusion.5
  342.6 2.3 fusion.93
  346.1 2.6 multiply_reduce_fusion.3
  349.1 2.5 fusion.90
  352.7 2.5 multiply_reduce_fusion.1
  355.7 2.3 fusion.87
  359.2 2.9 fusion.29
  363.3 2.3 fusion.111
  366.9 2.0 fusion.30
  369.5 12.9 %all_to_all.10 = bf16[4,64,1024]{2,1,0:T(8,128)(2,1)S(1)} all-to-all(bf16[4,64,1024]{2,1,0:T(8,128)(2,1)S(1)} %convert_element_type.62), channel_id=1, replica_groups=mesh['seq'=64,'head'=4] {'head'}, dimensions={0} | all-to-all | bytes 1048576 | tf_op jit(solution)/shard_map/all_to_all | solution.py:87
  (111 shorter events, 78.6 us)
Async XLA Ops:
  6.5 5.5 %copy-start = (bf16[256,1024]{1,0:T(8,128)(2,1)S(1)}, bf16[256,1024]{1,0:T(8,128)(2,1)}, u32[]{:S(2)}) copy-start(bf16[256,1024]{1,0:T(8,128)(2,1)} %param.11) | copy-start | bytes 1572868
  6.5 1.4 copy-start.1
  6.5 1.8 copy-start.3
  6.5 109.6 %all-gather.5.cloned.1.call-start = ((), (), s32[]{:S(2)}) async-start(), calls=%async_computation.1 | async-start | bytes 17039360 | tf_op jit(solution)/shard_map/all_gather | solution.py:15
  12.0 203.6 %all-gather.7.cloned.1.call-start = ((), (), s32[]{:S(2)}) async-start(), calls=%async_computation.2 | async-start | bytes 17039360 | tf_op jit(solution)/shard_map/all_gather | solution.py:15
  311.6 1.6 copy-start.2
  311.6 1.6 copy-start.5
  382.4 1.0 copy-start.4
  382.4 1.0 copy-start.6
Sparse Core Ops, SparseCore 0:
  12.2 103.8 all-gather.4
  118.9 96.7 all-gather.6
where the time goes:
time: 398 us; the launch traced here: 392 us
  waiting for transfers between devices  197 us (49%)
  other arithmetic  100 us (25%)
  matrix products  62.8 us (16%)
  between operations  14.4 us (4%)
  blocking collectives  12.9 us (3%)
    all_gather x2, waiting for transfers between devices, prefix(): lax.all_gather(part.astype(kind), axis)  197 us
    select_n x64, other arithmetic, turn(): return jax.tree.map(lambda a, b: jnp.where(reached, a, b), new, before)  94.3 us
    dot_general x8, matrix products, conj_grad(): jnp.einsum('hts,hsd->htd', weights * scores, key_n, precision=precise)  20.7 us
    dot_general x8, matrix products, conj_grad(): scores = jnp.einsum('htd,hsd->hts', direction, key_n, precision=precise)  20.4 us
    all_to_all x1, blocking collectives, shards(): lax.all_to_all(mesa_out, 'head', split_axis=0, concat_axis=1, tiled=True)  12.9 us
    dot_general x8, matrix products, conj_grad(): carried = jnp.einsum('htd,hde->hte', direction, prev_kk, precision=precise)  9.22 us
  transfers between devices with their start and end apart: 2, of which 2 were waited for; matrix products, arithmetic and copies ran while one was open for 2% of the time, Pallas kernels for 0%

commit v1 on v0

v1 whole, which is shorter than its diff:
```python
import functools

import jax
import jax.numpy as jnp
from jax import lax
from jax.experimental import pallas as pl
from jax.experimental.pallas import tpu as pltpu
from jax.sharding import PartitionSpec as P

MESH = pl.DeviceIdType.MESH
f32, bf16 = jnp.float32, jnp.bfloat16
ITERS = 8
HEADS = 8
DH = 128
TOK = 256
ROW = 8
COL = 8
Y = 4
ROWS_OUT = TOK // Y
EPS = 1e-6
GROUP = 4


def dot(a, b):
    return jnp.dot(a, b, preferred_element_type=f32)


def sums(x):
    return jnp.sum(x, axis=0, keepdims=True)


def split(x):
    hi = x.astype(bf16)
    return hi, (x - hi.astype(f32)).astype(bf16)


def stack(x):
    return jnp.concatenate(split(x), axis=0)


def iota(shape, axis):
    return lax.broadcasted_iota(jnp.int32, shape, axis)


def weigh(scores, top_left, top_right, bottom_right):
    top = jnp.concatenate([scores[0:128, 0:128] * top_left, scores[0:128, 128:256] * top_right], axis=1)
    bottom = jnp.concatenate([jnp.zeros((128, 128), f32), scores[128:256, 128:256] * bottom_right], axis=1)
    return jnp.concatenate([top, bottom], axis=0)


def diag_rows(d):
    hi = d.astype(bf16).astype(f32)
    row = iota((16, 128), 0)
    return jnp.where(row == 0, hi, jnp.where(row == 1, d - hi, 0.0)).astype(bf16)


def diag_of(rows):
    return rows[0:1] + rows[1:2]


def kernel(
    q, k, v, wg, ridge, gain, gate, out,
    keys2, mix, kt, vt, w, cvb, r, p, x, rr, dgb, sg, mesa, full,
    snd_k, row_k, ebuf_k, cs_k, cr_k, zs_k, zr_k, s4_k, all_k,
    snd_v, row_v, ebuf_v, cs_v, cr_v, zs_v, zr_v, s4_v, all_v,
    ssem, rsem, ysend, yrecv,
):
    seq, y = lax.axis_index("seq"), lax.axis_index("head")
    z, me = seq // ROW, seq % ROW

    def row_peer(i):
        return (me + i) % ROW

    def col_peer(i):
        return (z + i) % COL

    barrier = pltpu.get_barrier_semaphore()
    for i in range(1, ROW):
        pl.semaphore_signal(barrier, inc=1, device_id=(z * ROW + row_peer(i), y), device_id_type=MESH)
    for i in range(1, COL):
        pl.semaphore_signal(barrier, inc=1, device_id=(col_peer(i) * ROW + me, y), device_id_type=MESH)
    for i in range(1, Y):
        pl.semaphore_signal(barrier, inc=1, device_id=(seq, (y + i) % Y), device_id_type=MESH)

    started = []

    def send(stage, i, src, dst, in_row):
        to = z * ROW + row_peer(i) if in_row else col_peer(i) * ROW + me
        copy = pltpu.make_async_remote_copy(
            src_ref=src,
            dst_ref=dst,
            send_sem=ssem.at[stage, i - 1],
            recv_sem=rsem.at[stage, i - 1],
            device_id=(to, y),
            device_id_type=MESH,
        )
        copy.start()
        started.append(copy)
        return copy

    eye = iota((128, 128), 0) == iota((128, 128), 1)
    tri = iota((128, 128), 0) <= iota((128, 128), 1)
    lane8 = iota((TOK, HEADS), 1)

    wait_k1, wait_v1 = [], []
    for i in list(range(1, ROW)) + [0]:
        h = row_peer(i)
        cols = pl.ds(pl.multiple_of(h * DH, DH), DH)
        kb = k[:, cols]
        k32 = kb.astype(f32)
        inv = lax.rsqrt(jnp.sum(k32 * k32, axis=1, keepdims=True) + EPS)
        b = jnp.sum(jnp.where(lane8 == h, wg[...], 0.0), axis=1, keepdims=True)
        cv = b * inv
        c = cv * inv
        k_t = k32.T.astype(bf16)
        state = dot(k_t, (k32 * c).astype(bf16))
        snd_k[h, 0:128] = jnp.where(eye, 0.0, state).astype(bf16)
        snd_k[h, 128:144] = diag_rows(sums(jnp.where(eye, state, 0.0)))
        if i == 1:
            pl.semaphore_wait(barrier, ROW + COL + Y - 3)
        if i:
            wait_k1.append(send(0, i, snd_k.at[h], row_k.at[me], True))
        else:
            row_k[me] = snd_k[me]
        keys2[h, :, 0:128] = kb
        keys2[h, :, 128:256] = kb
        kt[h] = k_t
        w[h, 0] = jnp.where(tri, c[0:128], 0.0)
        w[h, 1] = jnp.broadcast_to(c[0:128], (128, 128))
        w[h, 2] = jnp.where(tri, c[128:256], 0.0)
        cvb[h] = jnp.broadcast_to(cv, (TOK, DH))
    for i in list(range(1, ROW)) + [0]:
        h = row_peer(i)
        cols = pl.ds(pl.multiple_of(h * DH, DH), DH)
        v_t = v[:, cols].astype(f32).T.astype(bf16)
        vt[h] = v_t
        snd_v[h] = dot(v_t, (k[:, cols].astype(f32) * cvb[h]).astype(bf16)).astype(bf16)
        if i:
            wait_v1.append(send(1, i, snd_v.at[h], row_v.at[me], True))
        else:
            row_v[me] = snd_v[me]

    def row_sums(waits, rows, ebuf, pieces, landed, stage, with_diag):
        for copy in waits:
            copy.wait_recv()
        total = jnp.zeros(ebuf.shape[1:], f32)
        for s in range(ROW):
            ebuf[s] = total
            total = total + rows[s].astype(f32)
        for j in range(COL):
            pieces[j, 0:16] = total[16 * j : 16 * j + 16].astype(bf16)
            if with_diag:
                pieces[j, 16:32] = diag_rows(diag_of(total[128:144]))
        landed[z] = pieces[z]
        return [send(stage, i, pieces.at[col_peer(i)], landed.at[z], False) for i in range(1, COL)]

    def col_sums(waits, landed, zs, zr, stage):
        for copy in waits:
            copy.wait_recv()
        total = jnp.zeros((16, 128), f32)
        for s in range(COL):
            zs[s] = total.astype(bf16)
            total = total + landed[s, 0:16].astype(f32)
        zr[z] = zs[z]
        return [send(stage, i, zs.at[col_peer(i)], zr.at[z], False) for i in range(1, COL)]

    def hand_out(waits, zr, ebuf, s4, everything, stage, diag):
        for copy in waits:
            copy.wait_recv()
        before = jnp.concatenate([zr[j].astype(f32) for j in range(COL)], axis=0)
        copies = []
        for i in list(range(1, ROW)) + [0]:
            to = row_peer(i)
            s4[to, 0:128] = (before + ebuf[to, 0:128]).astype(bf16)
            if diag is not None:
                s4[to, 128:144] = diag_rows(diag + diag_of(ebuf[to, 128:144]))
            if i:
                copies.append(send(stage, i, s4.at[to], everything.at[me], True))
            else:
                everything[me] = s4[me]
        return copies

    def normalized_queries(heads):
        for h in heads:
            q32 = q[:, h * DH : (h + 1) * DH].astype(f32)
            q_t = (q32 * lax.rsqrt(jnp.sum(q32 * q32, axis=1, keepdims=True) + EPS)).T
            r[h] = q_t
            p[h] = q_t
            rr[h] = jnp.broadcast_to(sums(q_t * q_t), (8, TOK))

    wait_k2 = row_sums(wait_k1, row_k, ebuf_k, cs_k, cr_k, 2, True)
    normalized_queries(range(0, 4))
    wait_v2 = row_sums(wait_v1, row_v, ebuf_v, cs_v, cr_v, 3, False)
    wait_k3 = col_sums(wait_k2, cr_k, zs_k, zr_k, 4)
    normalized_queries(range(4, 8))
    diag = jnp.zeros((1, 128), f32)
    for s in range(COL):
        diag = diag + jnp.where(s < z, diag_of(cr_k[s, 16:32].astype(f32)), 0.0)
    wait_v3 = col_sums(wait_v2, cr_v, zs_v, zr_v, 5)
    for j in range(Y):
        part = slice(1024 * j, 1024 * j + 1024)
        sg[:, part] = gain[:, part] * jax.nn.sigmoid(gate[:, part].astype(f32))
    wait_k4 = hand_out(wait_k3, zr_k, ebuf_k, s4_k, all_k, 6, diag)
    wait_v4 = hand_out(wait_v3, zr_v, ebuf_v, s4_v, all_v, 7, None)

    for copy in wait_k4:
        copy.wait_recv()
    for h in range(HEADS):
        before = all_k[h, 0:128]
        mix[h, :, 0:128] = before
        mix[h, :, 128:256] = before
        mix[h, :, 256:512] = kt[h]
        d = diag_of(all_k[h, 128:144].astype(f32)) + ridge[h : h + 1]
        dgb[h] = jnp.broadcast_to(jnp.sum(jnp.where(eye, d, 0.0), axis=1, keepdims=True), (128, 128))

    def apply(h, direction):
        pp = stack(direction)
        inner = weigh(dot(keys2[h], pp), w[h, 0], w[h, 1], w[h, 2]).astype(bf16)
        d = dgb[h]
        return dot(mix[h], jnp.concatenate([pp, inner], axis=0)) + jnp.concatenate([d, d], axis=1) * direction

    wait_y = []
    for group in range(HEADS // GROUP):
        heads = range(group * GROUP, (group + 1) * GROUP)

        def sweep(step, carry, heads=heads):
            images = [apply(h, p[h]) for h in heads]
            for h, image in zip(heads, images):
                direction, norm_now = p[h], rr[h][0:1]
                alpha = norm_now / sums(direction * image)
                x[h] = jnp.where(step == 0, 0.0, x[h]) + alpha * direction
                residual = r[h] - alpha * image
                r[h] = residual
                norm_next = sums(residual * residual)
                p[h] = residual + (norm_next / norm_now) * direction
                rr[h] = jnp.broadcast_to(norm_next, (8, TOK))
            return carry

        lax.fori_loop(0, ITERS - 1, sweep, 0)
        if group == 0:
            for copy in wait_v4:
                copy.wait_recv()
        for h in heads:
            direction = p[h]
            alpha = rr[h][0:1] / sums(direction * apply(h, direction))
            xx = stack(x[h] + alpha * direction)
            cv = cvb[h]
            top = cv[0:128]
            scores = weigh(dot(keys2[h], xx), jnp.where(tri, top, 0.0), top, jnp.where(tri, cv[128:256], 0.0))
            hi, lo = split(scores)
            before = all_v[h]
            mesa_t = dot(jnp.concatenate([before, before], axis=1), xx) + dot(vt[h], hi) + dot(vt[h], lo)
            mesa[:, h * DH : (h + 1) * DH] = mesa_t.T.astype(bf16)
        cols = slice(group * GROUP * DH, (group + 1) * GROUP * DH)
        for i in range(1, Y):
            to = (y + i) % Y
            copy = pltpu.make_async_remote_copy(
                src_ref=mesa.at[pl.ds(pl.multiple_of(to * ROWS_OUT, ROWS_OUT), ROWS_OUT), cols],
                dst_ref=full.at[y, :, cols],
                send_sem=ysend.at[group, i - 1],
                recv_sem=yrecv.at[group, i - 1],
                device_id=(seq, to),
                device_id_type=MESH,
            )
            copy.start()
            wait_y.append(copy)
    full[y] = mesa[pl.ds(pl.multiple_of(y * ROWS_OUT, ROWS_OUT), ROWS_OUT), :]
    for copy in wait_y:
        copy.wait_recv()
    square = jnp.zeros((ROWS_OUT, 1), f32)
    for j in range(Y):
        part = full[j].astype(f32)
        square = square + jnp.sum(part * part, axis=1, keepdims=True)
    factor = lax.rsqrt(square * (1.0 / (Y * HEADS * DH)) + EPS)
    for j in range(Y):
        cols = slice(1024 * j, 1024 * j + 1024)
        out[:, cols] = (full[j].astype(f32) * factor * sg[:, cols]).astype(bf16)
    for copy in started + wait_y:
        copy.wait_send()


def shards(queries, key_rows, values, write_gate, ridge_diag, norm_gain, gate_logits):
    V = pltpu.VMEM
    D = Y * HEADS * DH

    def comm(rows, piece):
        return [
            V((ROW, rows, 128), bf16),
            V((ROW, rows, 128), bf16),
            V((ROW, rows, 128), f32),
            V((COL, piece, 128), bf16),
            V((COL, piece, 128), bf16),
            V((COL, 16, 128), bf16),
            V((COL, 16, 128), bf16),
            V((ROW, rows, 128), bf16),
            V((ROW, rows, 128), bf16),
        ]

    state = V((HEADS, DH, TOK), f32)
    return pl.pallas_call(
        kernel,
        out_shape=jax.ShapeDtypeStruct((ROWS_OUT, D), bf16),
        in_specs=[pl.BlockSpec(memory_space=pltpu.VMEM)] * 7,
        out_specs=pl.BlockSpec(memory_space=pltpu.VMEM),
        scratch_shapes=[
            V((HEADS, TOK, 2 * DH), bf16),
            V((HEADS, DH, 4 * DH), bf16),
            V((HEADS, DH, TOK), bf16),
            V((HEADS, DH, TOK), bf16),
            V((HEADS, 3, 128, 128), f32),
            V((HEADS, TOK, DH), f32),
            state,
            state,
            state,
            V((HEADS, 8, TOK), f32),
            V((HEADS, DH, DH), f32),
            V((ROWS_OUT, D), f32),
            V((TOK, HEADS * DH), bf16),
            V((Y, ROWS_OUT, HEADS * DH), bf16),
            *comm(144, 32),
            *comm(128, 16),
            pltpu.SemaphoreType.DMA((8, 7)),
            pltpu.SemaphoreType.DMA((8, 7)),
            pltpu.SemaphoreType.DMA((HEADS // GROUP, 3)),
            pltpu.SemaphoreType.DMA((HEADS // GROUP, 3)),
        ],
        compiler_params=pltpu.CompilerParams(
            collective_id=0, has_side_effects=True, vmem_limit_bytes=48 << 20
        ),
    )(queries, key_rows, values, write_gate, ridge_diag, norm_gain.reshape(1, D), gate_logits)


def solution(mesh):
    return jax.shard_map(
        shards,
        mesh=mesh,
        in_specs=(
            P("seq", "head"),
            P("seq", "head"),
            P("seq", "head"),
            P("seq", "head"),
            P("head", None),
            P(),
            P(("seq", "head"), None),
        ),
        out_specs=P(("seq", "head"), None),
        check_vma=False,
    )
```

time: 398 us -> 60.9 us (0.15); the launches traced: 392 us -> 60.6 us
  waiting for transfers between devices: 197 us -> 0 us
  other arithmetic: 100 us -> 0 us
  matrix products: 62.8 us -> 0 us
  Pallas kernels: 0 us -> 54.7 us
  between operations: 14.4 us -> 0.05 us
  blocking collectives: 12.9 us -> 0 us
    all_gather x2 -> x0, waiting for transfers between devices: 197 us -> none  [prefix(): lax.all_gather(part.astype(kind), axis)]
    select_n x64 -> x0, other arithmetic: 94.3 us -> none  [turn(): return jax.tree.map(lambda a, b: jnp.where(reached, a, b), new, before)]
    dot_general x29 -> x0, matrix products: 62.8 us -> none  [the longest x8 20.7 us: conj_grad(): jnp.einsum('hts,hsd->htd', weights * scores, key_n, precision=precise)]
    pallas_call x0 -> x1, Pallas kernels: none -> 54.7 us  [shards(): pl.pallas_call(kernel, out_shape=jax.ShapeDtypeStruct((ROWS_OUT, D), bf16...]
    all_to_all x1 -> x0, blocking collectives: 12.9 us -> none  [shards(): lax.all_to_all(mesa_out, 'head', split_axis=0, concat_axis=1, tiled=True)]
    unnamed x14, local copies, waits for them, and re-layouts: 1.03 us -> 5.81 us
  transfers between devices with their start and end apart: 2 -> 0, of which waited for: 2 -> 0; matrix products, arithmetic and copies ran while one was open for 2% -> 0% of each run, Pallas kernels for 0% -> 0%
where the time goes in v1:
time: 60.9 us; the launch traced here: 60.6 us
  Pallas kernels  54.7 us (90%)
  local copies, waits for them, and re-layouts  5.81 us (10%)
    pallas_call x1, Pallas kernels, shards(): pl.pallas_call(kernel, out_shape=jax.ShapeDtypeStruct((ROWS_OUT, D), bf16...  54.7 us
    unnamed x14, local copies, waits for them, and re-layouts  5.81 us

profile of v1, /device:TPU:1, one launch (start us, length us, event | category | flops | bytes accessed | tf_op | source)
XLA Modules:
  0.0 60.6 jit_solution(11607649604343457363)
XLA Ops:
  0.0 0.0 copy-start.4
  0.0 0.0 copy-start.5
  0.0 0.8 %copy.8.wg = f32[256,8]{1,0:T(8,128)S(1)} copy(f32[256,8]{0,1:T(8,128)} %param.10) | data formatting | bytes 16384 | tf_op args[3]
  0.9 0.0 copy-done.4
  0.9 0.0 copy-done.5
  0.9 0.0 copy-start
  0.9 1.0 %copy-done = bf16[256,1024]{1,0:T(8,128)(2,1)S(1)} copy-done((bf16[256,1024]{1,0:T(8,128)(2,1)S(1)}, bf16[256,1024]{1,0:T(8,128)(2,1)}, u32[]{:S(2)}) %copy-start) | copy-done | bytes 524312
  1.9 0.0 copy-start.1
  1.9 1.0 %copy-done.1 = bf16[256,1024]{1,0:T(8,128)(2,1)S(1)} copy-done((bf16[256,1024]{1,0:T(8,128)(2,1)S(1)}, bf16[256,1024]{1,0:T(8,128)(2,1)}, u32[]{:S(2)}) %copy-start.1) | copy-done | bytes 524312
  3.0 0.0 copy-start.2
  3.0 1.0 %copy-done.2 = bf16[256,1024]{1,0:T(8,128)(2,1)S(1)} copy-done((bf16[256,1024]{1,0:T(8,128)(2,1)S(1)}, bf16[256,1024]{1,0:T(8,128)(2,1)}, u32[]{:S(2)}) %copy-start.2) | copy-done | bytes 524312
  4.0 0.0 copy-start.3
  4.0 1.0 %copy-done.3 = bf16[64,4096]{1,0:T(8,128)(2,1)S(1)} copy-done((bf16[64,4096]{1,0:T(8,128)(2,1)S(1)}, bf16[64,4096]{1,0:T(8,128)(2,1)}, u32[]{:S(2)}) %copy-start.3) | copy-done | bytes 524312
  5.0 54.7 %shard_map.73 = bf16[64,4096]{1,0:T(8,128)(2,1)S(1)} custom-call(bf16[256,1024]{1,0:T(8,128)(2,1)S(1)} %copy-done, bf16[256,1024]{1,0:T(8,128)(2,1)S(1)} %copy-done.1, bf16[256,1024]{1,0:T(8,128)(2,1)S(1)} %copy-done.2, f32[256,8]{1,0:T(8,128)S(1)} %copy.8.wg, f32[8,128]{1,0:T(8,128)S(1)} %copy-done.5, f32[1,4096]{1,0:T(1,128)S(1)} %bitcast.1, ...), custom_call_target="tpu_custom_call" | custom-call | tf_op jit(solution)/shard_map/pallas_call | solution.py:300
  59.8 0.8 %copy.10 = bf16[64,4096]{1,0:T(8,128)(2,1)} copy(bf16[64,4096]{1,0:T(8,128)(2,1)S(1)} %shard_map.73) | data formatting | bytes 1048576
Async XLA Ops:
  0.0 0.9 %copy-start.4 = (f32[4096]{0:T(1024)S(1)}, f32[4096]{0:T(1024)}, u32[]{:S(2)}) copy-start(f32[4096]{0:T(1024)} %param.12) | copy-start | bytes 49156
  0.0 0.9 %copy-start.5 = (f32[8,128]{1,0:T(8,128)S(1)}, f32[8,128]{1,0:T(8,128)}, u32[]{:S(2)}) copy-start(f32[8,128]{1,0:T(8,128)} %ridge.1) | copy-start | bytes 12292
  0.9 1.0 %copy-start = (bf16[256,1024]{1,0:T(8,128)(2,1)S(1)}, bf16[256,1024]{1,0:T(8,128)(2,1)}, u32[]{:S(2)}) copy-start(bf16[256,1024]{1,0:T(8,128)(2,1)} %q.1) | copy-start | bytes 1572868
  1.9 1.0 %copy-start.1 = (bf16[256,1024]{1,0:T(8,128)(2,1)S(1)}, bf16[256,1024]{1,0:T(8,128)(2,1)}, u32[]{:S(2)}) copy-start(bf16[256,1024]{1,0:T(8,128)(2,1)} %k.1) | copy-start | bytes 1572868
  3.0 1.0 %copy-start.2 = (bf16[256,1024]{1,0:T(8,128)(2,1)S(1)}, bf16[256,1024]{1,0:T(8,128)(2,1)}, u32[]{:S(2)}) copy-start(bf16[256,1024]{1,0:T(8,128)(2,1)} %v.1) | copy-start | bytes 1572868
  4.0 1.0 %copy-start.3 = (bf16[64,4096]{1,0:T(8,128)(2,1)S(1)}, bf16[64,4096]{1,0:T(8,128)(2,1)}, u32[]{:S(2)}) copy-start(bf16[64,4096]{1,0:T(8,128)(2,1)} %gate.1) | copy-start | bytes 1572868

commit v2 on v0

v2 whole, which is shorter than its diff:
```python
import functools

import jax
import jax.numpy as jnp
from jax import lax
from jax.experimental import pallas as pl
from jax.experimental.pallas import tpu as pltpu
from jax.sharding import PartitionSpec as P

MESH = pl.DeviceIdType.MESH
f32, bf16 = jnp.float32, jnp.bfloat16
ITERS = 8
HEADS = 8
DH = 128
TOK = 256
ROW = 8
COL = 8
Y = 4
QUARTER = TOK // Y
D = Y * HEADS * DH
EPS = 1e-6
FIRST, LAST = (0, 1), (2, 3, 6, 7, 4, 5)
FINISH = ((0, 1, 2, 3), (6, 7, 4, 5))


def dot(a, b):
    return jnp.dot(a, b, preferred_element_type=f32)


def sums(x):
    return jnp.sum(x, axis=0, keepdims=True)


def split(x):
    hi = x.astype(bf16)
    return hi, (x - hi.astype(f32)).astype(bf16)


def stack(x):
    return jnp.concatenate(split(x), axis=0)


def iota(shape, axis):
    return lax.broadcasted_iota(jnp.int32, shape, axis)


def causal(scores, tri):
    top = jnp.concatenate([jnp.where(tri, scores[0:128, 0:128], 0.0), scores[0:128, 128:256]], axis=1)
    bottom = jnp.concatenate(
        [jnp.zeros((128, 128), f32), jnp.where(tri, scores[128:256, 128:256], 0.0)], axis=1
    )
    return jnp.concatenate([top, bottom], axis=0)


def diag_rows(d):
    hi = d.astype(bf16).astype(f32)
    row = iota((16, 128), 0)
    return jnp.where(row == 0, hi, jnp.where(row == 1, d - hi, 0.0)).astype(bf16)


def diag_of(rows):
    return rows[0:1] + rows[1:2]


def flip(a, s):
    for bit in (1, 2, 4):
        if s & bit:
            a = a + bit - 2 * bit * ((a // bit) % 2)
    return a


def kernel(
    q, k, v, wgt, ridge, gain, gate, out,
    kbuf, qbuf, vbuf, wbuf, rbuf, nbuf, gbuf,
    keys2, mix, gg, vct, r, p, x, rr, cvs, dgb, sg, mesa, full,
    snd_k, row_k, e_k, cs_k, cr_k, zs_k, zr_k, s4_k, all_k,
    snd_v, row_v, e_v, cs_v, cr_v, zs_v, zr_v, s4_v, all_v,
    rs_s, rs_r, cs_s, cs_r, os_s, os_r, loc,
):
    seq, y = lax.axis_index("seq"), lax.axis_index("head")
    z, me = seq // ROW, seq % ROW
    heads = [flip(me, s) for s in range(HEADS)]

    barrier = pltpu.get_barrier_semaphore()
    for i in range(1, ROW):
        pl.semaphore_signal(barrier, inc=1, device_id=(z * ROW + heads[i], y), device_id_type=MESH)
    for i in range(1, COL):
        pl.semaphore_signal(barrier, inc=1, device_id=(flip(z, i) * ROW + me, y), device_id_type=MESH)
    for i in range(1, Y):
        pl.semaphore_signal(barrier, inc=1, device_id=(seq, flip(y, i)), device_id_type=MESH)

    def columns(ref, s):
        return ref.at[:, pl.ds(pl.multiple_of(heads[s] * DH, DH), DH)]

    local = {}

    def fetch(name, src, dst):
        local[name] = pltpu.make_async_copy(src, dst, loc.at[len(local)])
        local[name].start()

    fetch("w", wgt, wbuf)
    for s in ORDER:
        fetch(("k", s), columns(k, s), kbuf.at[s])
    started = []

    def start(src, dst, ssem, rsem, device):
        copy = pltpu.make_async_remote_copy(
            src_ref=src, dst_ref=dst, send_sem=ssem, recv_sem=rsem, device_id=device, device_id_type=MESH
        )
        copy.start()
        started.append(copy)
        return copy

    def to_row(stage, s, src, dst):
        sems = rs_s.at[stage, s - 1], rs_r.at[stage, s - 1]
        return start(src.at[s], dst.at[s], *sems, (z * ROW + heads[s], y))

    def to_col(stage, src, dst):
        return [
            start(
                src.at[flip(z, i)],
                dst.at[z],
                cs_s.at[stage, i - 1],
                cs_r.at[stage, i - 1],
                (flip(z, i) * ROW + me, y),
            )
            for i in range(1, COL)
        ]

    eye = iota((128, 128), 0) == iota((128, 128), 1)
    tri = iota((128, 128), 0) <= iota((128, 128), 1)

    local["w"].wait()
    wait_k1 = []
    for s in ORDER:
        local["k", s].wait()
        kb = kbuf[s]
        k_t = kb.astype(f32).T
        inv = lax.rsqrt(sums(k_t * k_t) + EPS)
        cv = wbuf[pl.ds(heads[s], 1), :] * inv
        kc_t = (k_t * (cv * inv)).astype(bf16)
        state = dot(kc_t, kb)
        snd_k[s, 0:128] = jnp.where(eye, 0.0, state).astype(bf16)
        snd_k[s, 128:144] = diag_rows(sums(jnp.where(eye, state, 0.0)))
        if s == ORDER[0]:
            pl.semaphore_wait(barrier, ROW + COL + Y - 3)
        if s:
            wait_k1.append(to_row(0, s, snd_k, row_k))
            fetch(("v", s), columns(v, s), vbuf.at[s])
        else:
            row_k[0] = snd_k[0]
            fetch(("v", 0), columns(v, 0), vbuf.at[0])
        cvs[s] = jnp.broadcast_to(cv, (8, TOK))
        mix[s, :, 256:512] = kc_t
    for s in range(HEADS):
        fetch(("q", s), columns(q, s), qbuf.at[s])
    fetch("r", ridge, rbuf)
    fetch("n", gain, nbuf)
    fetch("g", gate, gbuf)
    wait_v1 = []
    for s in ORDER:
        local["v", s].wait()
        vc_t = (vbuf[s].astype(f32).T * cvs[s, 0:1]).astype(bf16)
        vct[s] = vc_t
        snd_v[s] = dot(vc_t, kbuf[s]).astype(bf16)
        if s:
            wait_v1.append(to_row(1, s, snd_v, row_v))
        else:
            row_v[0] = snd_v[0]

    def row_sums(waits, rows, e, pieces, landed, stage, with_diag):
        for copy in waits:
            copy.wait_recv()
        total = rows[0].astype(f32)
        for b in range(1, ROW):
            total = total + rows[b].astype(f32)
        tail = diag_rows(diag_of(total[128:144])) if with_diag else None
        for j in range(COL):
            pieces[j, 0:16] = total[16 * j : 16 * j + 16].astype(bf16)
            if with_diag:
                pieces[j, 16:32] = tail
        landed[z] = pieces[z]
        copies = to_col(stage, pieces, landed)
        total = jnp.zeros(e.shape[1:], f32)
        for b in range(ROW):
            e[b] = total
            if b < ROW - 1:
                total = total + rows[flip(me, b)].astype(f32)
        return copies

    def col_sums(waits, landed, zs, zr, stage):
        for copy in waits:
            copy.wait_recv()
        total = jnp.zeros((16, 128), f32)
        for b in range(COL):
            zs[b] = total.astype(bf16)
            total = total + landed[b, 0:16].astype(f32)
        zr[z] = zs[z]
        return to_col(stage, zs, zr)

    def hand_out(waits, zr, e, s4, everything, stage, diag):
        for copy in waits:
            copy.wait_recv()
        before = jnp.concatenate([zr[j].astype(f32) for j in range(COL)], axis=0)
        copies = {}
        for s in (1, 4, 5, 2, 3, 6, 7, 0):
            row = e[heads[s]]
            s4[s, 0:128] = (before + row[0:128]).astype(bf16)
            if diag is not None:
                s4[s, 128:144] = diag_rows(diag + diag_of(row[128:144]))
            if s:
                copies[s] = to_row(stage, s, s4, everything)
            else:
                everything[0] = s4[0]
        return copies

    wait_k2 = row_sums(wait_k1, row_k, e_k, cs_k, cr_k, 0, True)

    for s in range(HEADS):
        local["q", s].wait()
        q_t = qbuf[s].astype(f32).T
        q_t = q_t * lax.rsqrt(sums(q_t * q_t) + EPS)
        r[s] = q_t
        p[s] = q_t
        x[s] = jnp.zeros((DH, TOK), f32)
        rr[s] = jnp.broadcast_to(sums(q_t * q_t), (8, TOK))
        keys2[s, :, 0:128] = kbuf[s]
        keys2[s, :, 128:256] = kbuf[s]
    wait_v2 = row_sums(wait_v1, row_v, e_v, cs_v, cr_v, 1, False)

    wait_k3 = col_sums(wait_k2, cr_k, zs_k, zr_k, 2)
    diag = jnp.zeros((1, 128), f32)
    for b in range(COL):
        diag = diag + jnp.where(b < z, diag_of(cr_k[b, 16:32].astype(f32)), 0.0)
    for name in ("r", "n", "g"):
        local[name].wait()
    for j in range(Y):
        part = slice(1024 * j, 1024 * j + 1024)
        sg[:, part] = nbuf[:, part] * jax.nn.sigmoid(gbuf[:, part].astype(f32))
    wait_v3 = col_sums(wait_v2, cr_v, zs_v, zr_v, 3)
    wait_k4 = hand_out(wait_k3, zr_k, e_k, s4_k, all_k, 2, diag)

    def apply(s, direction):
        pp = stack(direction)
        inner = causal(dot(keys2[s], pp), tri).astype(bf16)
        d = dgb[s]
        return dot(mix[s], jnp.concatenate([pp, inner], axis=0)) + jnp.concatenate([d, d], axis=1) * direction

    def solve(slots):
        for s in slots:
            if s:
                wait_k4[s].wait_recv()
            before = all_k[s, 0:128]
            mix[s, :, 0:128] = before
            mix[s, :, 128:256] = before
            d = diag_of(all_k[s, 128:144].astype(f32)) + rbuf[pl.ds(heads[s], 1), :]
            dgb[s] = jnp.broadcast_to(jnp.sum(jnp.where(eye, d, 0.0), axis=1, keepdims=True), (128, 128))

        def sweep(step, carry):
            images = [apply(s, p[s]) for s in slots]
            for s, image in zip(slots, images):
                direction, norm_now = p[s], rr[s][0:1]
                alpha = norm_now / sums(direction * image)
                x[s] = x[s] + alpha * direction
                residual = r[s] - alpha * image
                r[s] = residual
                norm_next = sums(residual * residual)
                p[s] = residual + (norm_next / norm_now) * direction
                rr[s] = jnp.broadcast_to(norm_next, (8, TOK))
            return carry

        lax.fori_loop(0, ITERS - 1, sweep, 0, unroll=True)

    wait_out = []

    def finish(slots):
        for s in slots:
            if s:
                wait_v4[s].wait_recv()
            gg[s, :, 0:128] = all_v[s]
            gg[s, :, 128:256] = all_v[s]
        images = [apply(s, p[s]) for s in slots]
        found = [stack(x[s] + (rr[s][0:1] / sums(p[s] * image)) * p[s]) for s, image in zip(slots, images)]
        scores = [causal(dot(keys2[s], xx), tri).astype(bf16) for s, xx in zip(slots, found)]
        results = [
            dot(jnp.concatenate([gg[s], vct[s]], axis=1), jnp.concatenate([xx, inner], axis=0))
            for s, xx, inner in zip(slots, found, scores)
        ]
        for s, result in zip(slots, results):
            mesa[s] = result.T.astype(bf16)
        for s in slots:
            for i in range(1, Y):
                to = flip(y, i)
                wait_out.append(
                    start(
                        mesa.at[s, pl.ds(pl.multiple_of(to * QUARTER, QUARTER), QUARTER), :],
                        full.at[y, heads[s]],
                        os_s.at[s, i - 1],
                        os_r.at[s, i - 1],
                        (seq, to),
                    )
                )
            full[y, heads[s]] = mesa[s, pl.ds(pl.multiple_of(y * QUARTER, QUARTER), QUARTER), :]

    solve(FIRST)
    wait_v4 = hand_out(wait_v3, zr_v, e_v, s4_v, all_v, 3, None)
    solve(LAST)
    for slots in FINISH:
        finish(slots)

    for copy in wait_out:
        copy.wait_recv()
    square = jnp.zeros((QUARTER, DH), f32)
    for j in range(Y):
        for h in range(HEADS):
            part = full[j, h].astype(f32)
            square = square + part * part
    factor = lax.rsqrt(jnp.sum(square, axis=1, keepdims=True) * (1.0 / D) + EPS)
    for j in range(Y):
        for h in range(HEADS):
            cols = slice((j * HEADS + h) * DH, (j * HEADS + h + 1) * DH)
            out[:, cols] = (full[j, h].astype(f32) * factor * sg[:, cols]).astype(bf16)
    for copy in started:
        copy.wait_send()


ORDER = (4, 5, 2, 3, 6, 7, 1, 0)


def shards(queries, key_rows, values, write_gate, ridge_diag, norm_gain, gate_logits):
    V = pltpu.VMEM
    raw = V((HEADS, TOK, DH), bf16)
    state = V((HEADS, DH, TOK), f32)
    col = V((COL, 16, DH), bf16)
    wide = V((COL, 32, DH), bf16)

    def comm(rows, piece):
        sent = V((ROW, rows, DH), bf16)
        return sent, sent, V((ROW, rows, DH), f32), piece, piece, col, col, sent, sent

    hbm, vmem = pl.BlockSpec(memory_space=pltpu.HBM), pl.BlockSpec(memory_space=pltpu.VMEM)
    return pl.pallas_call(
        kernel,
        out_shape=jax.ShapeDtypeStruct((QUARTER, D), bf16),
        in_specs=[hbm] * 7,
        out_specs=vmem,
        scratch_shapes=[
            raw,
            raw,
            raw,
            V((HEADS, TOK), f32),
            V((HEADS, DH), f32),
            V((1, D), f32),
            V((QUARTER, D), bf16),
            V((HEADS, TOK, 2 * DH), bf16),
            V((HEADS, DH, 4 * DH), bf16),
            V((HEADS, DH, 2 * DH), bf16),
            V((HEADS, DH, TOK), bf16),
            state,
            state,
            state,
            V((HEADS, 8, TOK), f32),
            V((HEADS, 8, TOK), f32),
            V((HEADS, DH, DH), f32),
            V((QUARTER, D), f32),
            raw,
            V((Y, HEADS, QUARTER, DH), bf16),
            *comm(144, wide),
            *comm(128, col),
            pltpu.SemaphoreType.DMA((4, 7)),
            pltpu.SemaphoreType.DMA((4, 7)),
            pltpu.SemaphoreType.DMA((4, 7)),
            pltpu.SemaphoreType.DMA((4, 7)),
            pltpu.SemaphoreType.DMA((HEADS, Y - 1)),
            pltpu.SemaphoreType.DMA((HEADS, Y - 1)),
            pltpu.SemaphoreType.DMA((28,)),
        ],
        compiler_params=pltpu.CompilerParams(
            collective_id=0, has_side_effects=True, vmem_limit_bytes=56 << 20
        ),
    )(queries, key_rows, values, write_gate.T, ridge_diag, norm_gain.reshape(1, D), gate_logits)


def solution(mesh):
    return jax.shard_map(
        shards,
        mesh=mesh,
        in_specs=(
            P("seq", "head"),
            P("seq", "head"),
            P("seq", "head"),
            P("seq", "head"),
            P("head", None),
            P(),
            P(("seq", "head"), None),
        ),
        out_specs=P(("seq", "head"), None),
        check_vma=False,
    )
```

time: 398 us -> 50.8 us (0.13); the launches traced: 392 us -> 50.7 us
  waiting for transfers between devices: 197 us -> 0 us
  other arithmetic: 100 us -> 0 us
  matrix products: 62.8 us -> 0 us
  Pallas kernels: 0 us -> 48.8 us
  between operations: 14.4 us -> 0.01 us
  blocking collectives: 12.9 us -> 0 us
    all_gather x2 -> x0, waiting for transfers between devices: 197 us -> none  [prefix(): lax.all_gather(part.astype(kind), axis)]
    select_n x64 -> x0, other arithmetic: 94.3 us -> none  [turn(): return jax.tree.map(lambda a, b: jnp.where(reached, a, b), new, before)]
    dot_general x29 -> x0, matrix products: 62.8 us -> none  [the longest x8 20.7 us: conj_grad(): jnp.einsum('hts,hsd->htd', weights * scores, key_n, precision=precise)]
    pallas_call x0 -> x1, Pallas kernels: none -> 48.8 us  [shards(): pl.pallas_call(kernel, out_shape=jax.ShapeDtypeStruct((QUARTER, D), bf16)...]
    all_to_all x1 -> x0, blocking collectives: 12.9 us -> none  [shards(): lax.all_to_all(mesa_out, 'head', split_axis=0, concat_axis=1, tiled=True)]
  transfers between devices with their start and end apart: 2 -> 0, of which waited for: 2 -> 0; matrix products, arithmetic and copies ran while one was open for 2% -> 0% of each run, Pallas kernels for 0% -> 0%
where the time goes in v2:
time: 50.8 us; the launch traced here: 50.7 us
  Pallas kernels  48.8 us (96%)
  local copies, waits for them, and re-layouts  1.87 us (4%)
    pallas_call x1, Pallas kernels, shards(): pl.pallas_call(kernel, out_shape=jax.ShapeDtypeStruct((QUARTER, D), bf16)...  48.8 us
    unnamed x1, local copies, waits for them, and re-layouts  1.87 us

profile of v2, /device:TPU:1, one launch (start us, length us, event | category | flops | bytes accessed | tf_op | source)
XLA Modules:
  0.0 50.7 jit_solution(10164837044522310857)
XLA Ops:
  0.0 48.8 %shard_map.73 = bf16[64,4096]{1,0:T(8,128)(2,1)} custom-call(bf16[256,1024]{1,0:T(8,128)(2,1)} %q.1, bf16[256,1024]{1,0:T(8,128)(2,1)} %k.1, bf16[256,1024]{1,0:T(8,128)(2,1)} %v.1, f32[8,256]{1,0:T(8,128)} %bitcast.3, f32[8,128]{1,0:T(8,128)} %ridge.1, f32[1,4096]{1,0:T(1,128)} %bitcast.2, bf16[64,4096]{1,0:T(8,128)(2,1)} %gate.1), custom_call_target="tpu_custom_call" | custom-call | tf_op jit(solution)/shard_map/pallas_call | solution.py:342
  48.8 1.9 %copy.9 = bf16[64,4096]{1,0:T(8,128)(2,1)} copy(bf16[64,4096]{1,0:T(8,128)(2,1)} %shard_map.73) | data formatting | bytes 1048576

commit v3 on v2

--- a/solution.py
+++ b/solution.py
@@ -20,7 +20,7 @@
 D = Y * HEADS * DH
 EPS = 1e-6
 FIRST, LAST = (0, 1), (2, 3, 6, 7, 4, 5)
-FINISH = ((0, 1, 2, 3), (6, 7, 4, 5))
+FINISH = ((2, 3, 6), (7, 4, 5))
 
 
 def dot(a, b):
@@ -67,6 +67,19 @@
         if s & bit:
             a = a + bit - 2 * bit * ((a // bit) % 2)
     return a
+
+
+def pack(state):
+    row, lane = iota((64, 128), 0), iota((64, 128), 1)
+    low = pltpu.roll(state[64:128], 64, 1)
+    return jnp.where(lane > row, state[0:64], jnp.where(lane < row, low, 0.0))
+
+
+def unpack(half):
+    row, lane = iota((64, 128), 0), iota((64, 128), 1)
+    low = pltpu.roll(jnp.where(lane < row, half, 0.0), 64, 1)
+    upper = jnp.concatenate([jnp.where(lane > row, half, 0.0), low], axis=0)
+    return upper + upper.T
 
 
 def kernel(
@@ -132,41 +145,46 @@
 
     local["w"].wait()
     wait_k1 = []
-    for s in ORDER:
-        local["k", s].wait()
-        kb = kbuf[s]
-        k_t = kb.astype(f32).T
-        inv = lax.rsqrt(sums(k_t * k_t) + EPS)
-        cv = wbuf[pl.ds(heads[s], 1), :] * inv
-        kc_t = (k_t * (cv * inv)).astype(bf16)
-        state = dot(kc_t, kb)
-        snd_k[s, 0:128] = jnp.where(eye, 0.0, state).astype(bf16)
-        snd_k[s, 128:144] = diag_rows(sums(jnp.where(eye, state, 0.0)))
-        if s == ORDER[0]:
+    for batch in (ORDER[:4], ORDER[4:]):
+        for s in batch:
+            local["k", s].wait()
+        keys_t = [kbuf[s].astype(f32).T for s in batch]
+        invs = [lax.rsqrt(sums(k_t * k_t) + EPS) for k_t in keys_t]
+        gates = [wbuf[pl.ds(heads[s], 1), :] * inv for s, inv in zip(batch, invs)]
+        weighed = [(k_t * (cv * inv)).astype(bf16) for k_t, cv, inv in zip(keys_t, gates, invs)]
+        states = [dot(kc_t, kbuf[s]) for s, kc_t in zip(batch, weighed)]
+        for s, state in zip(batch, states):
+            snd_k[s, 0:64] = pack(state).astype(bf16)
+            snd_k[s, 64:80] = diag_rows(sums(jnp.where(eye, state, 0.0)))
+        for s, cv, kc_t in zip(batch, gates, weighed):
+            cvs[s] = jnp.broadcast_to(cv, (8, TOK))
+            mix[s, :, 256:512] = kc_t
+        if batch[0] == ORDER[0]:
             pl.semaphore_wait(barrier, ROW + COL + Y - 3)
-        if s:
-            wait_k1.append(to_row(0, s, snd_k, row_k))
+        for s in batch:
+            if s:
+                wait_k1.append(to_row(0, s, snd_k, row_k))
+        for s in batch:
             fetch(("v", s), columns(v, s), vbuf.at[s])
-        else:
-            row_k[0] = snd_k[0]
-            fetch(("v", 0), columns(v, 0), vbuf.at[0])
-        cvs[s] = jnp.broadcast_to(cv, (8, TOK))
-        mix[s, :, 256:512] = kc_t
+    row_k[0] = snd_k[0]
     for s in range(HEADS):
         fetch(("q", s), columns(q, s), qbuf.at[s])
     fetch("r", ridge, rbuf)
     fetch("n", gain, nbuf)
     fetch("g", gate, gbuf)
     wait_v1 = []
-    for s in ORDER:
-        local["v", s].wait()
-        vc_t = (vbuf[s].astype(f32).T * cvs[s, 0:1]).astype(bf16)
-        vct[s] = vc_t
-        snd_v[s] = dot(vc_t, kbuf[s]).astype(bf16)
-        if s:
-            wait_v1.append(to_row(1, s, snd_v, row_v))
-        else:
-            row_v[0] = snd_v[0]
+    for batch in (ORDER[:4], ORDER[4:]):
+        for s in batch:
+            local["v", s].wait()
+        weighed = [(vbuf[s].astype(f32).T * cvs[s, 0:1]).astype(bf16) for s in batch]
+        states = [dot(vc_t, kbuf[s]) for s, vc_t in zip(batch, weighed)]
+        for s, vc_t, state in zip(batch, weighed, states):
+            vct[s] = vc_t
+            snd_v[s] = state.astype(bf16)
+        for s in batch:
+            if s:
+                wait_v1.append(to_row(1, s, snd_v, row_v))
+    row_v[0] = snd_v[0]
 
     def row_sums(waits, rows, e, pieces, landed, stage, with_diag):
         for copy in waits:
@@ -174,11 +192,12 @@
         total = rows[0].astype(f32)
         for b in range(1, ROW):
             total = total + rows[b].astype(f32)
-        tail = diag_rows(diag_of(total[128:144])) if with_diag else None
         for j in range(COL):
-            pieces[j, 0:16] = total[16 * j : 16 * j + 16].astype(bf16)
             if with_diag:
-                pieces[j, 16:32] = tail
+                pieces[j, 0:8] = total[8 * j : 8 * j + 8]
+                pieces[j, 8:16] = jnp.broadcast_to(diag_of(total[64:80]), (8, 128))
+            else:
+                pieces[j] = total[16 * j : 16 * j + 16].astype(bf16)
         landed[z] = pieces[z]
         copies = to_col(stage, pieces, landed)
         total = jnp.zeros(e.shape[1:], f32)
@@ -191,10 +210,11 @@
     def col_sums(waits, landed, zs, zr, stage):
         for copy in waits:
             copy.wait_recv()
-        total = jnp.zeros((16, 128), f32)
+        rows = zs.shape[1]
+        total = jnp.zeros((rows, 128), f32)
         for b in range(COL):
-            zs[b] = total.astype(bf16)
-            total = total + landed[b, 0:16].astype(f32)
+            zs[b] = total.astype(zs.dtype)
+            total = total + landed[b, 0:rows].astype(f32)
         zr[z] = zs[z]
         return to_col(stage, zs, zr)
 
@@ -203,18 +223,21 @@
             copy.wait_recv()
         before = jnp.concatenate([zr[j].astype(f32) for j in range(COL)], axis=0)
         copies = {}
-        for s in (1, 4, 5, 2, 3, 6, 7, 0):
-            row = e[heads[s]]
-            s4[s, 0:128] = (before + row[0:128]).astype(bf16)
-            if diag is not None:
-                s4[s, 128:144] = diag_rows(diag + diag_of(row[128:144]))
-            if s:
-                copies[s] = to_row(stage, s, s4, everything)
-            else:
-                everything[0] = s4[0]
+        for batch in ((1, 4, 5, 2), (3, 6, 7, 0)):
+            for s in batch:
+                row = e[heads[s]]
+                rows = before.shape[0]
+                s4[s, 0:rows] = (before + row[0:rows]).astype(bf16)
+                if diag is not None:
+                    s4[s, 64:80] = diag_rows(diag + diag_of(row[64:80]))
+            for s in batch:
+                if s:
+                    copies[s] = to_row(stage, s, s4, everything)
+        everything[0] = s4[0]
         return copies
 
     wait_k2 = row_sums(wait_k1, row_k, e_k, cs_k, cr_k, 0, True)
+    wait_v2 = row_sums(wait_v1, row_v, e_v, cs_v, cr_v, 1, False)
 
     for s in range(HEADS):
         local["q", s].wait()
@@ -226,18 +249,16 @@
         rr[s] = jnp.broadcast_to(sums(q_t * q_t), (8, TOK))
         keys2[s, :, 0:128] = kbuf[s]
         keys2[s, :, 128:256] = kbuf[s]
-    wait_v2 = row_sums(wait_v1, row_v, e_v, cs_v, cr_v, 1, False)
-
     wait_k3 = col_sums(wait_k2, cr_k, zs_k, zr_k, 2)
+    wait_v3 = col_sums(wait_v2, cr_v, zs_v, zr_v, 3)
     diag = jnp.zeros((1, 128), f32)
     for b in range(COL):
-        diag = diag + jnp.where(b < z, diag_of(cr_k[b, 16:32].astype(f32)), 0.0)
+        diag = diag + jnp.where(b < z, cr_k[b, 8:9], 0.0)
     for name in ("r", "n", "g"):
         local[name].wait()
     for j in range(Y):
         part = slice(1024 * j, 1024 * j + 1024)
         sg[:, part] = nbuf[:, part] * jax.nn.sigmoid(gbuf[:, part].astype(f32))
-    wait_v3 = col_sums(wait_v2, cr_v, zs_v, zr_v, 3)
     wait_k4 = hand_out(wait_k3, zr_k, e_k, s4_k, all_k, 2, diag)
 
     def apply(s, direction):
@@ -246,48 +267,60 @@
         d = dgb[s]
         return dot(mix[s], jnp.concatenate([pp, inner], axis=0)) + jnp.concatenate([d, d], axis=1) * direction
 
-    def solve(slots):
+    def place_states(slots):
         for s in slots:
             if s:
                 wait_k4[s].wait_recv()
-            before = all_k[s, 0:128]
+            before = unpack(all_k[s, 0:64].astype(f32)).astype(bf16)
             mix[s, :, 0:128] = before
             mix[s, :, 128:256] = before
-            d = diag_of(all_k[s, 128:144].astype(f32)) + rbuf[pl.ds(heads[s], 1), :]
+            d = diag_of(all_k[s, 64:80].astype(f32)) + rbuf[pl.ds(heads[s], 1), :]
             dgb[s] = jnp.broadcast_to(jnp.sum(jnp.where(eye, d, 0.0), axis=1, keepdims=True), (128, 128))
 
-        def sweep(step, carry):
-            images = [apply(s, p[s]) for s in slots]
-            for s, image in zip(slots, images):
-                direction, norm_now = p[s], rr[s][0:1]
-                alpha = norm_now / sums(direction * image)
-                x[s] = x[s] + alpha * direction
-                residual = r[s] - alpha * image
-                r[s] = residual
-                norm_next = sums(residual * residual)
-                p[s] = residual + (norm_next / norm_now) * direction
-                rr[s] = jnp.broadcast_to(norm_next, (8, TOK))
+    def sweep(slots):
+        images = [apply(s, p[s]) for s in slots]
+        for s, image in zip(slots, images):
+            direction, norm_now = p[s], rr[s][0:1]
+            alpha = norm_now / sums(direction * image)
+            x[s] = x[s] + alpha * direction
+            residual = r[s] - alpha * image
+            r[s] = residual
+            norm_next = sums(residual * residual)
+            p[s] = residual + (norm_next / norm_now) * direction
+            rr[s] = jnp.broadcast_to(norm_next, (8, TOK))
+
+    def sweeps(slots, count):
+        def step(n, carry):
+            sweep(slots)
             return carry
 
-        lax.fori_loop(0, ITERS - 1, sweep, 0, unroll=True)
+        lax.fori_loop(0, count, step, 0, unroll=True)
 
     wait_out = []
 
-    def finish(slots):
+    def solution_of(slots):
+        images = [apply(s, p[s]) for s in slots]
+        return [stack(x[s] + (rr[s][0:1] / sums(p[s] * image)) * p[s]) for s, image in zip(slots, images)]
+
+    def attention(slots, found):
+        return [causal(dot(keys2[s], xx), tri).astype(bf16) for s, xx in zip(slots, found)]
+
+    def place_values(slots):
         for s in slots:
             if s:
                 wait_v4[s].wait_recv()
             gg[s, :, 0:128] = all_v[s]
             gg[s, :, 128:256] = all_v[s]
-        images = [apply(s, p[s]) for s in slots]
-        found = [stack(x[s] + (rr[s][0:1] / sums(p[s] * image)) * p[s]) for s, image in zip(slots, images)]
-        scores = [causal(dot(keys2[s], xx), tri).astype(bf16) for s, xx in zip(slots, found)]
-        results = [
-            dot(jnp.concatenate([gg[s], vct[s]], axis=1), jnp.concatenate([xx, inner], axis=0))
-            for s, xx, inner in zip(slots, found, scores)
+
+    def results(slots, found, inner):
+        outs = [
+            dot(jnp.concatenate([gg[s], vct[s]], axis=1), jnp.concatenate([xx, scores], axis=0))
+            for s, xx, scores in zip(slots, found, inner)
         ]
-        for s, result in zip(slots, results):
+        for s, result in zip(slots, outs):
             mesa[s] = result.T.astype(bf16)
+
+    def send_out(slots):
         for s in slots:
             for i in range(1, Y):
                 to = flip(y, i)
@@ -302,11 +335,24 @@
                 )
             full[y, heads[s]] = mesa[s, pl.ds(pl.multiple_of(y * QUARTER, QUARTER), QUARTER), :]
 
-    solve(FIRST)
     wait_v4 = hand_out(wait_v3, zr_v, e_v, s4_v, all_v, 3, None)
-    solve(LAST)
+    place_states(FIRST)
+    sweeps(FIRST, ITERS - 1)
+    place_states(LAST)
+    found = solution_of(FIRST)
+    sweep(LAST)
+    inner = attention(FIRST, found)
+    sweep(LAST)
+    place_values(FIRST)
+    results(FIRST, found, inner)
+    sweep(LAST)
+    send_out(FIRST)
+    sweeps(LAST, ITERS - 4)
+    place_values(LAST)
     for slots in FINISH:
-        finish(slots)
+        found = solution_of(slots)
+        results(slots, found, attention(slots, found))
+        send_out(slots)
 
     for copy in wait_out:
         copy.wait_recv()
@@ -332,11 +378,10 @@
     raw = V((HEADS, TOK, DH), bf16)
     state = V((HEADS, DH, TOK), f32)
     col = V((COL, 16, DH), bf16)
-    wide = V((COL, 32, DH), bf16)
-
-    def comm(rows, piece):
+
+    def comm(rows, piece, back):
         sent = V((ROW, rows, DH), bf16)
-        return sent, sent, V((ROW, rows, DH), f32), piece, piece, col, col, sent, sent
+        return sent, sent, V((ROW, rows, DH), f32), piece, piece, back, back, sent, sent
 
     hbm, vmem = pl.BlockSpec(memory_space=pltpu.HBM), pl.BlockSpec(memory_space=pltpu.VMEM)
     return pl.pallas_call(
@@ -365,8 +410,8 @@
             V((QUARTER, D), f32),
             raw,
             V((Y, HEADS, QUARTER, DH), bf16),
-            *comm(144, wide),
-            *comm(128, col),
+            *comm(80, V((COL, 16, DH), f32), V((COL, 8, DH), f32)),
+            *comm(128, col, col),
             pltpu.SemaphoreType.DMA((4, 7)),
             pltpu.SemaphoreType.DMA((4, 7)),
             pltpu.SemaphoreType.DMA((4, 7)),

time: 50.8 us -> 49.2 us (0.969)
  Pallas kernels: 48.8 us -> 47.1 us
    pallas_call x1, Pallas kernels: 48.8 us -> 47.1 us  [shards(): pl.pallas_call(kernel, out_shape=jax.ShapeDtypeStruct((QUARTER, D), bf16)...]
where the time goes in v3:
time: 49.2 us; the launch traced here: 48.9 us
  Pallas kernels  47.1 us (96%)
  local copies, waits for them, and re-layouts  1.87 us (4%)
    pallas_call x1, Pallas kernels, shards(): pl.pallas_call(kernel, out_shape=jax.ShapeDtypeStruct((QUARTER, D), bf16)...  47.1 us
    unnamed x1, local copies, waits for them, and re-layouts  1.87 us

profile of v3, /device:TPU:1, one launch (start us, length us, event | category | flops | bytes accessed | tf_op | source)
XLA Modules:
  0.0 48.9 jit_solution(2028009055978101650)
XLA Ops:
  0.0 47.1 %shard_map.73 = bf16[64,4096]{1,0:T(8,128)(2,1)} custom-call(bf16[256,1024]{1,0:T(8,128)(2,1)} %q.1, bf16[256,1024]{1,0:T(8,128)(2,1)} %k.1, bf16[256,1024]{1,0:T(8,128)(2,1)} %v.1, f32[8,256]{1,0:T(8,128)} %bitcast.3, f32[8,128]{1,0:T(8,128)} %ridge.1, f32[1,4096]{1,0:T(1,128)} %bitcast.2, bf16[64,4096]{1,0:T(8,128)(2,1)} %gate.1), custom_call_target="tpu_custom_call" | custom-call | tf_op jit(solution)/shard_map/pallas_call | solution.py:387
  47.1 1.9 %copy.9 = bf16[64,4096]{1,0:T(8,128)(2,1)} copy(bf16[64,4096]{1,0:T(8,128)(2,1)} %shard_map.73) | data formatting | bytes 1048576

commit v4 on v3

--- a/solution.py
+++ b/solution.py
@@ -20,7 +20,7 @@
 D = Y * HEADS * DH
 EPS = 1e-6
 FIRST, LAST = (0, 1), (2, 3, 6, 7, 4, 5)
-FINISH = ((2, 3, 6), (7, 4, 5))
+FINISH = ((2, 3), (6, 7), (4, 5))
 
 
 def dot(a, b):
@@ -271,6 +271,7 @@
         for s in slots:
             if s:
                 wait_k4[s].wait_recv()
+        for s in slots:
             before = unpack(all_k[s, 0:64].astype(f32)).astype(bf16)
             mix[s, :, 0:128] = before
             mix[s, :, 128:256] = before
@@ -322,7 +323,7 @@
 
     def send_out(slots):
         for s in slots:
-            for i in range(1, Y):
+            for i in (2, 1, 3):
                 to = flip(y, i)
                 wait_out.append(
                     start(
@@ -337,8 +338,10 @@
 
     wait_v4 = hand_out(wait_v3, zr_v, e_v, s4_v, all_v, 3, None)
     place_states(FIRST)
-    sweeps(FIRST, ITERS - 1)
+    sweeps(FIRST, ITERS - 3)
     place_states(LAST)
+    sweep(FIRST + LAST)
+    sweep(FIRST + LAST)
     found = solution_of(FIRST)
     sweep(LAST)
     inner = attention(FIRST, found)
@@ -347,20 +350,22 @@
     results(FIRST, found, inner)
     sweep(LAST)
     send_out(FIRST)
-    sweeps(LAST, ITERS - 4)
+    sweeps(LAST, ITERS - 6)
     place_values(LAST)
     for slots in FINISH:
         found = solution_of(slots)
         results(slots, found, attention(slots, found))
         send_out(slots)
 
-    for copy in wait_out:
-        copy.wait_recv()
     square = jnp.zeros((QUARTER, DH), f32)
-    for j in range(Y):
-        for h in range(HEADS):
-            part = full[j, h].astype(f32)
-            square = square + part * part
+    for slots in (FIRST, *FINISH):
+        for copy in wait_out[: 3 * len(slots)]:
+            copy.wait_recv()
+        del wait_out[: 3 * len(slots)]
+        for s in slots:
+            for i in range(Y):
+                part = full[flip(y, i), heads[s]].astype(f32)
+                square = square + part * part
     factor = lax.rsqrt(jnp.sum(square, axis=1, keepdims=True) * (1.0 / D) + EPS)
     for j in range(Y):
         for h in range(HEADS):

time: 49.2 us -> 47.6 us (0.967)
  Pallas kernels: 47.1 us -> 45.5 us
    pallas_call x1, Pallas kernels: 47.1 us -> 45.5 us  [shards(): pl.pallas_call(kernel, out_shape=jax.ShapeDtypeStruct((QUARTER, D), bf16)...]
where the time goes in v4:
time: 47.6 us; the launch traced here: 47.4 us
  Pallas kernels  45.5 us (96%)
  local copies, waits for them, and re-layouts  1.87 us (4%)
    pallas_call x1, Pallas kernels, shards(): pl.pallas_call(kernel, out_shape=jax.ShapeDtypeStruct((QUARTER, D), bf16)...  45.5 us
    unnamed x1, local copies, waits for them, and re-layouts  1.87 us

profile of v4, /device:TPU:1, one launch (start us, length us, event | category | flops | bytes accessed | tf_op | source)
XLA Modules:
  0.0 47.4 jit_solution(2469372580883166371)
XLA Ops:
  0.0 45.5 %shard_map.73 = bf16[64,4096]{1,0:T(8,128)(2,1)} custom-call(bf16[256,1024]{1,0:T(8,128)(2,1)} %q.1, bf16[256,1024]{1,0:T(8,128)(2,1)} %k.1, bf16[256,1024]{1,0:T(8,128)(2,1)} %v.1, f32[8,256]{1,0:T(8,128)} %bitcast.3, f32[8,128]{1,0:T(8,128)} %ridge.1, f32[1,4096]{1,0:T(1,128)} %bitcast.2, bf16[64,4096]{1,0:T(8,128)(2,1)} %gate.1), custom_call_target="tpu_custom_call" | custom-call | tf_op jit(solution)/shard_map/pallas_call | solution.py:392
  45.5 1.9 %copy.9 = bf16[64,4096]{1,0:T(8,128)(2,1)} copy(bf16[64,4096]{1,0:T(8,128)(2,1)} %shard_map.73) | data formatting | bytes 1048576

commit v5 on v4

--- a/solution.py
+++ b/solution.py
@@ -137,7 +137,7 @@
                 cs_r.at[stage, i - 1],
                 (flip(z, i) * ROW + me, y),
             )
-            for i in range(1, COL)
+            for i in (4, 5, 3, 6, 2, 1, 7)
         ]
 
     eye = iota((128, 128), 0) == iota((128, 128), 1)
@@ -145,7 +145,7 @@
 
     local["w"].wait()
     wait_k1 = []
-    for batch in (ORDER[:4], ORDER[4:]):
+    for batch in (ORDER[:3], ORDER[3:]):
         for s in batch:
             local["k", s].wait()
         keys_t = [kbuf[s].astype(f32).T for s in batch]
@@ -173,7 +173,7 @@
     fetch("n", gain, nbuf)
     fetch("g", gate, gbuf)
     wait_v1 = []
-    for batch in (ORDER[:4], ORDER[4:]):
+    for batch in (ORDER,):
         for s in batch:
             local["v", s].wait()
         weighed = [(vbuf[s].astype(f32).T * cvs[s, 0:1]).astype(bf16) for s in batch]

time: 47.6 us -> 45.2 us (0.950)
  Pallas kernels: 45.5 us -> 43 us
    pallas_call x1, Pallas kernels: 45.5 us -> 43 us  [shards(): pl.pallas_call(kernel, out_shape=jax.ShapeDtypeStruct((QUARTER, D), bf16)...]
where the time goes in v5:
time: 45.2 us; the launch traced here: 44.9 us
  Pallas kernels  43 us (95%)
  local copies, waits for them, and re-layouts  1.87 us (4%)
    pallas_call x1, Pallas kernels, shards(): pl.pallas_call(kernel, out_shape=jax.ShapeDtypeStruct((QUARTER, D), bf16)...  43 us
    unnamed x1, local copies, waits for them, and re-layouts  1.87 us

profile of v5, /device:TPU:1, one launch (start us, length us, event | category | flops | bytes accessed | tf_op | source)
XLA Modules:
  0.0 44.9 jit_solution(16896612298290948678)
XLA Ops:
  0.0 43.0 %shard_map.73 = bf16[64,4096]{1,0:T(8,128)(2,1)} custom-call(bf16[256,1024]{1,0:T(8,128)(2,1)} %q.1, bf16[256,1024]{1,0:T(8,128)(2,1)} %k.1, bf16[256,1024]{1,0:T(8,128)(2,1)} %v.1, f32[8,256]{1,0:T(8,128)} %bitcast.3, f32[8,128]{1,0:T(8,128)} %ridge.1, f32[1,4096]{1,0:T(1,128)} %bitcast.2, bf16[64,4096]{1,0:T(8,128)(2,1)} %gate.1), custom_call_target="tpu_custom_call" | custom-call | tf_op jit(solution)/shard_map/pallas_call | solution.py:392
  43.0 1.9 %copy.9 = bf16[64,4096]{1,0:T(8,128)(2,1)} copy(bf16[64,4096]{1,0:T(8,128)(2,1)} %shard_map.73) | data formatting | bytes 1048576

commit v6 on v5

--- a/solution.py
+++ b/solution.py
@@ -223,7 +223,7 @@
             copy.wait_recv()
         before = jnp.concatenate([zr[j].astype(f32) for j in range(COL)], axis=0)
         copies = {}
-        for batch in ((1, 4, 5, 2), (3, 6, 7, 0)):
+        for batch in ((1, 4, 5, 2, 3, 6, 7, 0),):
             for s in batch:
                 row = e[heads[s]]
                 rows = before.shape[0]
@@ -241,6 +241,7 @@
 
     for s in range(HEADS):
         local["q", s].wait()
+    for s in range(HEADS):
         q_t = qbuf[s].astype(f32).T
         q_t = q_t * lax.rsqrt(sums(q_t * q_t) + EPS)
         r[s] = q_t

time: 45.2 us -> 45.6 us (level)
  no operation moved by 1% of the time
where the time goes in v6:
time: 45.6 us; the launch traced here: 45.2 us
  Pallas kernels  43.3 us (95%)
  local copies, waits for them, and re-layouts  1.87 us (4%)
    pallas_call x1, Pallas kernels, shards(): pl.pallas_call(kernel, out_shape=jax.ShapeDtypeStruct((QUARTER, D), bf16)...  43.3 us
    unnamed x1, local copies, waits for them, and re-layouts  1.87 us

profile of v6, /device:TPU:1, one launch (start us, length us, event | category | flops | bytes accessed | tf_op | source)
XLA Modules:
  0.0 45.2 jit_solution(1018631104512498017)
XLA Ops:
  0.0 43.3 %shard_map.73 = bf16[64,4096]{1,0:T(8,128)(2,1)} custom-call(bf16[256,1024]{1,0:T(8,128)(2,1)} %q.1, bf16[256,1024]{1,0:T(8,128)(2,1)} %k.1, bf16[256,1024]{1,0:T(8,128)(2,1)} %v.1, f32[8,256]{1,0:T(8,128)} %bitcast.3, f32[8,128]{1,0:T(8,128)} %ridge.1, f32[1,4096]{1,0:T(1,128)} %bitcast.2, bf16[64,4096]{1,0:T(8,128)(2,1)} %gate.1), custom_call_target="tpu_custom_call" | custom-call | tf_op jit(solution)/shard_map/pallas_call | solution.py:393
  43.3 1.9 %copy.9 = bf16[64,4096]{1,0:T(8,128)(2,1)} copy(bf16[64,4096]{1,0:T(8,128)(2,1)} %shard_map.73) | data formatting | bytes 1048576
